TPU v7x, 32 devices: a whole 2x2x4 slice. The times are simulated.
32 devices in a mesh: groups: 2 (over y), video: 4 (over x, core), frame: 4 (over z).
Axes of the slice: x: 2, y: 2, z: 4, core: 2. Of those that a mesh axis runs over, the one named last changes fastest.
Arguments:
- latents: bfloat16 [8, 4, 256, 320], P(('groups', 'video'), 'frame'), parts along dimension 0, may hold values from -6 to 6
- timesteps: int32 [8], P(('groups', 'video')), parts along dimension 0, may hold values from 0 to 999
- matchings: int32 [2, 8], P(None, 'groups'), parts along dimension 1, may hold values from 0 to 3, each once within a row
- tile_mask: int32 [2, 8, 2, 2], P(None, 'groups'), parts along dimension 1, may hold values from 0 to 1, as said below
- conv_first: bfloat16 [3, 3, 320, 320], replicated, may hold values from -0.109375 to 0.109375
- conv_second: bfloat16 [3, 3, 320, 320], replicated, may hold values from -0.109375 to 0.109375
- time_proj: bfloat16 [1280, 320], P('frame'), may hold values from -0.15625 to 0.15625
- epi_in: bfloat16 [3, 320, 320], P(None, 'frame'), may hold values from -48 to 48
- epi_out: bfloat16 [320, 320], P('frame'), may hold values from -0.3125 to 0.3125
- temp_in: bfloat16 [3, 320, 320], P(None, 'frame'), may hold values from -48 to 48
- temp_out: bfloat16 [320, 320], P('frame'), may hold values from -0.3125 to 0.3125
Outputs:
- denoised: bfloat16 [8, 4, 256, 320], P(('groups', 'video'), 'frame'), parts along dimension 0
There are 2 independent parts, one for each index of `groups`. A program takes and returns all parts, laid end to end along the dimension named above; an argument that names none is the same for every part. Nothing has to cross between parts.
Inputs may be any that keep to these rules, and one draw needn't show every extreme that they name: Every row tile_mask[m, u, i, :] holds at least one 1.
All inputs are finite; a program needn't handle non-finite values.
Results may differ from a plain program's by a relative error of at most 0.035.
Values may be sent and summed in bfloat16 or wider, within the bound.
A program may use at most 64 MiB of HBM per device.

v0:
```python
import math

import jax
import jax.numpy as jnp
from jax import lax
from jax.sharding import PartitionSpec as P

HEADS = 8
NORM_GROUPS = 32
TEMB = 1280
H = 8
W = 32


epsilon = 1e-05
masked_fill = -1e30


def group_norm(values):
    row_count, channels = values.shape
    grouped = values.reshape(row_count, NORM_GROUPS, channels // NORM_GROUPS)
    average = jnp.mean(grouped, axis=(0, 2), keepdims=True)
    spread = jnp.mean(jnp.square(grouped - average), axis=(0, 2), keepdims=True)
    return ((grouped - average) / jnp.sqrt(spread + epsilon)).reshape(row_count, channels)


def layer_norm(values):
    average = jnp.mean(values, axis=-1, keepdims=True)
    spread = jnp.mean(jnp.square(values - average), axis=-1, keepdims=True)
    return (values - average) / jnp.sqrt(spread + epsilon)


def convolve(activations, weight):
    channels = activations.shape[-1]
    planar = activations.reshape(H, W, channels)
    padded = jnp.pad(planar, ((1, 1), (1, 1), (0, 0)))
    totals = jnp.zeros((H * W, weight.shape[-1]), jnp.float32)
    for row_shift in range(3):
        for col_shift in range(3):
            window = padded[row_shift : row_shift + H, col_shift : col_shift + W].reshape(
                H * W, channels
            )
            totals = totals + jnp.dot(
                window, weight[row_shift, col_shift], preferred_element_type=jnp.float32
            )
    return totals


def sinusoid(timestep):
    half_width = TEMB // 2
    frequency = jnp.exp(-math.log(10000.0) * jnp.arange(half_width, dtype=jnp.float32) / half_width)
    angles = timestep.astype(jnp.float32)[:, None] * frequency[None, :]
    return jnp.concatenate([jnp.cos(angles), jnp.sin(angles)], axis=-1)


def softmax_last(scores):
    maxima = jnp.max(scores, axis=-1, keepdims=True)
    powers = jnp.exp(scores - maxima)
    return powers / jnp.sum(powers, axis=-1, keepdims=True)


def epipolar(queries, key_rows, value_rows, pair_mask):
    row_count, channels = queries.shape
    tiles = pair_mask.shape[0]
    width = row_count // tiles
    split = (row_count, HEADS, channels // HEADS)
    scaling = 1.0 / math.sqrt(channels // HEADS)
    scores = (
        jnp.einsum(
            "qhd,khd->hqk",
            queries.reshape(split),
            key_rows.reshape(split),
            preferred_element_type=jnp.float32,
        )
        * scaling
    )
    scores = scores.reshape(HEADS, tiles, width, tiles, width)
    scores = jnp.where(pair_mask[None, :, None, :, None] > 0, scores, masked_fill)
    weights = softmax_last(scores.reshape(HEADS, row_count, row_count)).astype(jnp.bfloat16)
    result = jnp.einsum(
        "hqk,khd->qhd", weights, value_rows.reshape(split), preferred_element_type=jnp.float32
    )
    return result.reshape(row_count, channels)


def frame_attention(queries, key_rows, value_rows):
    frames, pixels, channels = queries.shape
    split = (frames, pixels, HEADS, channels // HEADS)
    scaling = 1.0 / math.sqrt(channels // HEADS)
    scores = (
        jnp.einsum(
            "fphd,gphd->phfg",
            queries.reshape(split),
            key_rows.reshape(split),
            preferred_element_type=jnp.float32,
        )
        * scaling
    )
    weights = softmax_last(scores).astype(jnp.bfloat16)
    result = jnp.einsum(
        "phfg,gphd->fphd", weights, value_rows.reshape(split), preferred_element_type=jnp.float32
    )
    return result.astype(jnp.bfloat16).reshape(frames, pixels, channels)


def project_block(blocks, weight):
    return jnp.einsum("fpc,cd->fpd", blocks, weight, preferred_element_type=jnp.float32).astype(
        jnp.bfloat16
    )


def per_device(
    latents,
    timesteps,
    matchings,
    tile_mask,
    conv_first,
    conv_second,
    time_proj,
    epi_in,
    epi_out,
    temp_in,
    temp_out,
):
    time_act = jax.nn.silu(sinusoid(timesteps)).astype(jnp.bfloat16)
    time_full, epi_whole, epi_final, temp_whole, temp_final = (
        lax.all_gather(time_proj, "frame", axis=0, tiled=True),
        lax.all_gather(epi_in, "frame", axis=1, tiled=True),
        lax.all_gather(epi_out, "frame", axis=0, tiled=True),
        lax.all_gather(temp_in, "frame", axis=1, tiled=True),
        lax.all_gather(temp_out, "frame", axis=0, tiled=True),
    )
    time_bias = jnp.dot(time_act, time_full, preferred_element_type=jnp.float32)
    tokens = latents.shape[2]
    channels = latents.shape[3]
    source = latents.reshape(tokens, channels)
    first_act = jax.nn.silu(group_norm(source.astype(jnp.float32))).astype(jnp.bfloat16)
    inner_sum = convolve(first_act, conv_first) + time_bias
    second_act = jax.nn.silu(group_norm(inner_sum)).astype(jnp.bfloat16)
    hidden = (source.astype(jnp.float32) + convolve(second_act, conv_second)).astype(jnp.bfloat16)
    normed = layer_norm(hidden.astype(jnp.float32)).astype(jnp.bfloat16)
    own_video = lax.axis_index("video")
    targets = matchings[:, own_video]
    shard_rows = lax.all_gather(normed.reshape(1, 1, tokens, channels), "video", axis=0, tiled=True)
    shard_count = shard_rows.shape[0]
    owners = jnp.arange(shard_count, dtype=jnp.int32)
    one_hot = (owners[None, :] == targets[:, None]).astype(jnp.bfloat16)
    selected = jnp.einsum(
        "mk,ktc->mtc", one_hot, shard_rows[:, 0], preferred_element_type=jnp.float32
    )
    matched = selected.astype(jnp.bfloat16)
    pair_masks = tile_mask[:, own_video]
    queries = jnp.dot(normed, epi_whole[0], preferred_element_type=jnp.float32).astype(jnp.bfloat16)
    key_all = jnp.einsum(
        "mtc,cd->mtd", matched, epi_whole[1], preferred_element_type=jnp.float32
    ).astype(jnp.bfloat16)
    value_all = jnp.einsum(
        "mtc,cd->mtd", matched, epi_whole[2], preferred_element_type=jnp.float32
    ).astype(jnp.bfloat16)
    summed = jnp.zeros((tokens, channels), jnp.float32)
    for matching in range(2):
        summed = summed + epipolar(
            queries, key_all[matching], value_all[matching], pair_masks[matching]
        )
    mixture = summed.astype(jnp.bfloat16)
    second_hidden = (
        hidden.astype(jnp.float32) + jnp.dot(mixture, epi_final, preferred_element_type=jnp.float32)
    ).astype(jnp.bfloat16)
    temp_normed = layer_norm(second_hidden.astype(jnp.float32)).astype(jnp.bfloat16)
    frames = lax.axis_size("frame")
    blocks = temp_normed.reshape(frames, tokens // frames, channels)
    regrouped = lax.all_to_all(blocks, "frame", split_axis=0, concat_axis=0, tiled=True)
    attended = frame_attention(
        project_block(regrouped, temp_whole[0]),
        project_block(regrouped, temp_whole[1]),
        project_block(regrouped, temp_whole[2]),
    )
    restored = lax.all_to_all(attended, "frame", split_axis=0, concat_axis=0, tiled=True)
    outcome = restored.reshape(tokens, channels)
    denoised = (
        second_hidden.astype(jnp.float32)
        + jnp.dot(outcome, temp_final, preferred_element_type=jnp.float32)
    ).astype(jnp.bfloat16)
    return denoised.reshape(1, 1, tokens, channels)


def solution(mesh):
    placed = (
        P(("groups", "video"), "frame", None, None),
        P(("groups", "video")),
        P(None, "groups"),
        P(None, "groups", None, None),
        P(),
        P(),
        P("frame", None),
        P(None, "frame", None),
        P("frame", None),
        P(None, "frame", None),
        P("frame", None),
    )
    return jax.shard_map(
        per_device,
        mesh=mesh,
        in_specs=placed,
        out_specs=P(("groups", "video"), "frame", None, None),
        check_vma=False,
    )
```

profile of v0, /device:TPU:0, one launch (start us, length us, event | category | flops | bytes accessed | tf_op | source)
XLA Modules:
  0.0 144.1 jit_solution(8931145181968467575)
XLA Ops:
  0.0 1.9 %copy.61 = f32[1,1,256,320]{3,2,1,0:T(8,128)} copy(bf16[1,1,256,320]{2,3,1,0:T(8,128)(2,1)} %param.11) | data formatting | bytes 491520 | tf_op jit(solution)/shard_map/convert_element_type | solution.py:140
  1.9 1.1 convert_reduce_fusion
  3.8 23.7 %all_gather.18 = bf16[1280,320]{1,0:T(8,128)(2,1)S(1)} all-gather(bf16[320,320]{1,0:T(8,128)(2,1)} %param.17), channel_id=1, replica_groups=mesh['groups'=2,'video'=4,'frame'=4] {'frame'}, dimensions={0}, use_global_device_ids=true | all-gather | bytes 1024000 | tf_op jit(solution)/shard_map/all_gather | solution.py:127
  27.9 1.1 fusion.27
  29.4 1.1 multiply_convert_fusion
  30.6 0.2 pad_slice_fusion.8
  30.8 0.3 fusion.48
  31.1 0.3 convolution_add_fusion.17
  31.4 0.3 convolution_add_fusion.16
  31.7 0.3 convolution_add_fusion.15
  32.0 0.4 convolution_add_fusion.14
  32.4 0.3 convolution_reduce_fusion
  32.7 0.3 convolution_add_fusion.13
  33.0 0.3 convolution_add_fusion.12
  33.3 0.3 convolution_add_fusion.11
  33.7 1.5 %fusion.92 = (f32[320]{0:T(512)S(1)}, f32[256,320]{0,1:T(8,128)S(1)}) fusion(f32[320]{0:T(512)S(1)} %convolution_reduce_fusion, f32[256,320]{0,1:T(8,128)S(1)} %convolution_add_fusion.11, bf16[256,320]{1,0:T(8,128)(2,1)S(1)} %bitcast.195, bf16[3,3,320,320]{3,2,1,0:T(8,128)(2,1)} %param.15), kind=kOutput, calls=%fused_computation.174 | convolution fusion | flops 52674240 | bytes 1067520 | tf_op jit(solution)/shard_map/dot_general | solution.py:43
  35.6 0.2 multiply_reduce_fusion.2
  36.2 0.2 multiply_convert_fusion.1
  36.8 0.3 fusion.38
  37.1 0.3 convolution_add_fusion.9
  37.4 0.3 convolution_add_fusion.8
  37.7 0.3 convolution_add_fusion.7
  38.0 0.3 convolution_add_fusion.6
  38.3 0.3 convolution_add_fusion.5
  38.6 0.3 convolution_add_fusion.4
  38.9 0.3 convolution_add_fusion.3
  39.3 0.3 fusion.93
  39.7 7.9 %all-gather = bf16[1024,320]{0,1:T(8,128)(2,1)S(1)} all-gather(bf16[256,320]{0,1:T(8,128)(2,1)S(1)} %divide_convert_fusion.7), channel_id=2, replica_groups=mesh['groups'=2,'video'=4,'frame'=4] {'video'}, dimensions={0}, use_global_device_ids=true | all-gather | bytes 819200 | tf_op jit(solution)/shard_map/all_gather | solution.py:144
  47.6 0.5 squeeze.94
  48.1 18.0 %all_gather.20 = bf16[3,320,320]{2,1,0:T(8,128)(2,1)S(1)} all-gather(bf16[3,80,320]{2,1,0:T(8,128)(2,1)S(1)} %copy-done.4), channel_id=1, replica_groups=mesh['groups'=2,'video'=4,'frame'=4] {'frame'}, dimensions={1}, use_global_device_ids=true | all-gather | bytes 768000 | tf_op jit(solution)/shard_map/all_gather | solution.py:128
  66.0 0.3 convolution_convert_fusion.7
  66.4 0.2 dynamic-slice_reduce_fusion
  66.6 0.6 convolution_convert_fusion.3
  67.1 0.4 convolution_convert_fusion.2
  67.5 0.4 convolution_convert_fusion.1
  67.9 0.2 compare_reduce_fusion
  68.3 0.2 copy.65
  68.7 0.2 copy.69
  68.9 14.5 %all_gather.21 = bf16[320,320]{1,0:T(8,128)(2,1)S(1)} all-gather(bf16[80,320]{1,0:T(8,128)(2,1)S(1)} %copy-done.6), channel_id=1, replica_groups=mesh['groups'=2,'video'=4,'frame'=4] {'frame'}, dimensions={0}, use_global_device_ids=true | all-gather | bytes 256000 | tf_op jit(solution)/shard_map/all_gather | solution.py:129
  83.4 2.2 %fusion.94 = (f32[8,256]{1,0:T(8,128)S(1)}, f32[8,256,256]{1,2,0:T(8,128)}) fusion(pred[256,256]{0,1:T(8,128)(4,1)S(1)} %copy.65, bf16[256,8,40]{0,2,1:T(8,128)(2,1)S(1)} %bitcast.218, bf16[256,8,40]{0,2,1:T(8,128)(2,1)S(1)} %bitcast.216), kind=kOutput, calls=%fused_computation.176 | convolution fusion | flops 44040448 | bytes 2498560 | tf_op jit(solution)/shard_map/sub | solution.py:58
  85.7 2.2 %fusion.95 = (f32[8,256]{1,0:T(8,128)S(1)}, f32[8,256,256]{1,2,0:T(8,128)}) fusion(pred[256,256]{0,1:T(8,128)(4,1)S(1)} %copy.69, bf16[256,8,40]{0,2,1:T(8,128)(2,1)S(1)} %bitcast.219, bf16[256,8,40]{0,2,1:T(8,128)(2,1)S(1)} %bitcast.215), kind=kOutput, calls=%fused_computation.177 | convolution fusion | flops 44040448 | bytes 2498560 | tf_op jit(solution)/shard_map/sub | solution.py:58
  87.8 2.0 %fusion.23 = f32[8,40,256]{2,1,0:T(8,128)S(1)} fusion(bf16[256,8,40]{0,2,1:T(8,128)(2,1)S(1)} %bitcast.214, f32[8,256,256]{1,2,0:T(8,128)} %get-tuple-element.32, f32[8,256]{1,0:T(8,128)S(1)} %get-tuple-element.31), kind=kOutput, calls=%fused_computation.59 | convolution fusion | flops 42991616 | bytes 2596864 | tf_op jit(solution)/shard_map/hqk,khd->qhd/dot_general | solution.py:80
  89.9 0.2 copy-done.9
  90.0 0.3 fusion.15
  90.4 0.3 fusion.96
  90.8 0.8 copy.71
  91.6 3.4 %all-to-all-start = ((bf16[4,64,320]{2,1,0:T(8,128)(2,1)}), bf16[4,64,320]{2,1,0:T(8,128)(2,1)S(1)}, u32[]{:S(2)}, u32[]{:S(2)}) async-start(bf16[4,64,320]{2,1,0:T(8,128)(2,1)} %bitcast.53), calls=%async_computation | async-start | bytes 393216 | tf_op jit(solution)/shard_map/all_to_all | solution.py:172
  95.0 19.5 %all_gather.22 = bf16[3,320,320]{2,1,0:T(8,128)(2,1)S(1)} all-gather(bf16[3,80,320]{2,1,0:T(8,128)(2,1)S(1)} %copy-done.5), channel_id=1, replica_groups=mesh['groups'=2,'video'=4,'frame'=4] {'frame'}, dimensions={1}, use_global_device_ids=true | all-gather | bytes 768000 | tf_op jit(solution)/shard_map/all_gather | solution.py:130
  114.5 0.3 convolution_convert_fusion.6
  114.8 0.2 copy.72
  115.0 0.8 copy.77
  115.8 0.3 convolution_convert_fusion.5
  116.1 0.2 copy.73
  116.3 0.8 copy.75
  117.1 0.3 convolution_convert_fusion.4
  117.4 0.2 copy.74
  117.6 0.8 copy.76
  118.4 2.7 %fusion.97 = (f32[64,8,4]{2,1,0:T(8,128)S(1)}, f32[64,8,4,4]{2,3,1,0:T(4,128)}) fusion(bf16[4,64,8,40]{3,0,2,1:T(4,128)(2,1)S(1)} %copy.75, bf16[4,64,8,40]{3,0,2,1:T(4,128)(2,1)S(1)} %copy.76), kind=kOutput, calls=%fused_computation.179 | convolution fusion | flops 679939 | bytes 368640 | tf_op jit(solution)/shard_map/sub | solution.py:58
  121.1 2.0 %fusion.7 = bf16[4,64,8,40]{3,0,2,1:T(4,128)(2,1)S(1)} fusion(bf16[4,64,8,40]{3,0,2,1:T(4,128)(2,1)S(1)} %copy.77, f32[64,8,4,4]{2,3,1,0:T(4,128)} %get-tuple-element.38, f32[64,8,4]{2,1,0:T(8,128)S(1)} %get-tuple-element.37), kind=kOutput, calls=%fused_computation.15 | convolution fusion | flops 753664 | bytes 368640 | tf_op jit(solution)/shard_map/phfg,gphd->fphd/dot_general | solution.py:100
  123.1 0.6 copy.79
  123.7 0.8 copy.80
  124.6 3.4 %all-to-all-start.1 = ((bf16[4,64,320]{2,1,0:T(8,128)(2,1)}), bf16[4,64,320]{2,1,0:T(8,128)(2,1)S(1)}, u32[]{:S(2)}, u32[]{:S(2)}) async-start(bf16[4,64,320]{2,1,0:T(8,128)(2,1)} %copy.80), calls=%async_computation.1 | async-start | bytes 393216 | tf_op jit(solution)/shard_map/all_to_all | solution.py:178
  128.0 15.1 %all_gather.23 = bf16[320,320]{1,0:T(8,128)(2,1)S(1)} all-gather(bf16[80,320]{1,0:T(8,128)(2,1)S(1)} %copy-done.7), channel_id=1, replica_groups=mesh['groups'=2,'video'=4,'frame'=4] {'frame'}, dimensions={0}, use_global_device_ids=true | all-gather | bytes 256000 | tf_op jit(solution)/shard_map/all_gather | solution.py:131
  143.1 1.0 fusion.16
  (60 shorter events, 2.7 us)
Async XLA Ops:
  0.0 66.4 %copy-start = (s32[2,4]{1,0:T(2,128)S(1)}, s32[2,4]{1,0:T(2,128)}, u32[]{:S(2)}) copy-start(s32[2,4]{1,0:T(2,128)} %param.13) | copy-start | bytes 100
  0.0 30.8 %copy-start.3 = (bf16[3,3,320,320]{3,2,1,0:T(8,128)(2,1)S(1)}, bf16[3,3,320,320]{3,2,1,0:T(8,128)(2,1)}, u32[]{:S(2)}) copy-start(bf16[3,3,320,320]{3,2,1,0:T(8,128)(2,1)} %param.15) | copy-start | bytes 5529604
  30.7 1.3 copy-start.1
  33.6 3.1 %copy-start.2 = (bf16[3,3,320,320]{3,2,1,0:T(8,128)(2,1)S(1)}, bf16[3,3,320,320]{3,2,1,0:T(8,128)(2,1)}, u32[]{:S(2)}) copy-start(bf16[3,3,320,320]{3,2,1,0:T(8,128)(2,1)} %param.16) | copy-start | bytes 5529604
  39.2 8.8 %copy-start.4 = (bf16[3,80,320]{2,1,0:T(8,128)(2,1)S(1)}, bf16[3,80,320]{2,1,0:T(8,128)(2,1)}, u32[]{:S(2)}) copy-start(bf16[3,80,320]{2,1,0:T(8,128)(2,1)} %param.18) | copy-start | bytes 460804
  66.3 1.6 %copy-start.8 = (s32[2,4,2,2]{1,3,2,0:T(2,128)S(1)}, s32[2,4,2,2]{1,3,2,0:T(2,128)}, u32[]{:S(2)}) copy-start(s32[2,4,2,2]{1,3,2,0:T(2,128)} %param.14) | copy-start | bytes 388
  67.1 1.8 %copy-start.6 = (bf16[80,320]{1,0:T(8,128)(2,1)S(1)}, bf16[80,320]{1,0:T(8,128)(2,1)}, u32[]{:S(2)}) copy-start(bf16[80,320]{1,0:T(8,128)(2,1)} %param.19) | copy-start | bytes 153604
  87.8 2.2 %copy-start.9 = (f32[8,256,256]{1,2,0:T(8,128)S(1)}, f32[8,256,256]{1,2,0:T(8,128)}, u32[]{:S(2)}) copy-start(f32[8,256,256]{1,2,0:T(8,128)} %get-tuple-element.34) | copy-start | bytes 6291460
  90.3 4.6 %copy-start.5 = (bf16[3,80,320]{2,1,0:T(8,128)(2,1)S(1)}, bf16[3,80,320]{2,1,0:T(8,128)(2,1)}, u32[]{:S(2)}) copy-start(bf16[3,80,320]{2,1,0:T(8,128)(2,1)} %param.20) | copy-start | bytes 460804
  91.6 22.9 %all-to-all-start = ((bf16[4,64,320]{2,1,0:T(8,128)(2,1)}), bf16[4,64,320]{2,1,0:T(8,128)(2,1)S(1)}, u32[]{:S(2)}, u32[]{:S(2)}) async-start(bf16[4,64,320]{2,1,0:T(8,128)(2,1)} %bitcast.53), calls=%async_computation | async-start | bytes 393216 | tf_op jit(solution)/shard_map/all_to_all | solution.py:172
  121.1 6.9 %copy-start.7 = (bf16[80,320]{1,0:T(8,128)(2,1)S(1)}, bf16[80,320]{1,0:T(8,128)(2,1)}, u32[]{:S(2)}) copy-start(bf16[80,320]{1,0:T(8,128)(2,1)} %param.21) | copy-start | bytes 153604
  124.6 18.5 %all-to-all-start.1 = ((bf16[4,64,320]{2,1,0:T(8,128)(2,1)}), bf16[4,64,320]{2,1,0:T(8,128)(2,1)S(1)}, u32[]{:S(2)}, u32[]{:S(2)}) async-start(bf16[4,64,320]{2,1,0:T(8,128)(2,1)} %copy.80), calls=%async_computation.1 | async-start | bytes 393216 | tf_op jit(solution)/shard_map/all_to_all | solution.py:178
where the time goes:
time: 145 us; the launch traced here: 144 us
  blocking collectives  98.7 us (68%)
  matrix products  22.1 us (15%)
  local copies, waits for them, and re-layouts  10.5 us (7%)
  starting transfers between devices  6.73 us (5%)
  other arithmetic  4.76 us (3%)
    all_gather x1, blocking collectives, per_device(): lax.all_gather(time_proj, 'frame', axis=0, tiled=True)  23.7 us
    all_gather x1, blocking collectives, per_device(): lax.all_gather(temp_in, 'frame', axis=1, tiled=True)  19.5 us
    all_gather x1, blocking collectives, per_device(): lax.all_gather(epi_in, 'frame', axis=1, tiled=True)  18 us
    all_gather x1, blocking collectives, per_device(): lax.all_gather(temp_out, 'frame', axis=0, tiled=True)  15.1 us
    all_gather x1, blocking collectives, per_device(): lax.all_gather(epi_out, 'frame', axis=0, tiled=True)  14.5 us
    all_gather x1, blocking collectives, per_device(): lax.all_gather(normed.reshape(1, 1, tokens, channels), 'video', axis=0, t...  7.88 us
    sub x3, matrix products, softmax_last(): powers = jnp.exp(scores - maxima)  7.07 us
    dot_general x18, matrix products, convolve(): jnp.dot(window, weight[row_shift, col_shift], preferred_element_type=jnp....  6.75 us
  transfers between devices with their start and end apart: 2, of which 0 were waited for; matrix products, arithmetic and copies ran while one was open for 0% of the time, Pallas kernels for 0%

commit v1 on v0

v1 whole, which is shorter than its diff:
```python
import functools
import math

import jax
import jax.numpy as jnp
from jax import lax
from jax.experimental import pallas as pl
from jax.experimental.pallas import tpu as pltpu
from jax.sharding import PartitionSpec as P

HEADS = 8
NORM_GROUPS = 32
TEMB = 1280
H = 8
W = 32
EPS = 1e-05
FILL = -1e30
F32 = jnp.float32
BF16 = jnp.bfloat16
MESH = pl.DeviceIdType.MESH


def dot(a, b):
    return jnp.dot(a, b, preferred_element_type=F32)


def dot_nt(a, b):
    return lax.dot_general(a, b, (((1,), (1,)), ((), ())), preferred_element_type=F32)


def iota(shape, dim):
    return lax.broadcasted_iota(jnp.int32, shape, dim)


def split_rows(row):
    hi = row.astype(BF16).astype(F32)
    rest = row - hi
    mid = rest.astype(BF16).astype(F32)
    low = rest - mid
    which = iota((16, row.shape[1]), 0)
    packed = jnp.where(which == 0, hi, jnp.where(which == 1, mid, jnp.where(which == 2, low, 0.0)))
    return packed.astype(BF16)


def group_total(row, same_group):
    return jnp.sum(dot(split_rows(row), same_group), axis=0, keepdims=True)


def gn_silu(values, same_group, count):
    average = group_total(jnp.sum(values, axis=0, keepdims=True), same_group) * (1.0 / count)
    centered = values - average
    spread = group_total(jnp.sum(centered * centered, axis=0, keepdims=True), same_group) * (
        1.0 / count
    )
    u = centered * (1.0 / jnp.sqrt(spread + EPS))
    return u * (1.0 / (1.0 + jnp.exp(-u)))


def layer_norm(values):
    average = jnp.mean(values, axis=-1, keepdims=True)
    centered = values - average
    spread = jnp.mean(centered * centered, axis=-1, keepdims=True)
    return centered * (1.0 / jnp.sqrt(spread + EPS))


def wave(angle, quarter_shift):
    n = jnp.floor(angle * (2.0 / math.pi) + 0.5)
    r = ((angle - n * 1.5703125) - n * 4.837512969970703125e-4) - n * 7.54978995489188216e-8
    z = r * r
    sin_r = r + r * z * (
        -1.6666654611e-1 + z * (8.3321608736e-3 + z * -1.9515295891e-4)
    )
    cos_r = (
        1.0
        - 0.5 * z
        + z * z * (4.166664568298827e-2 + z * (-1.388731625493765e-3 + z * 2.443315711809948e-5))
    )
    q = n + quarter_shift
    q = q - 4.0 * jnp.floor(q * 0.25)
    return jnp.where(
        q < 0.5, cos_r, jnp.where(q < 1.5, -sin_r, jnp.where(q < 2.5, -cos_r, sin_r))
    )


def kernel(
    frames,
    videos,
    chunks,
    steps_ref,
    match_ref,
    mask_ref,
    x_hbm,
    conv_a_hbm,
    conv_b_hbm,
    time_hbm,
    epi_in_hbm,
    epi_out_hbm,
    temp_in_hbm,
    temp_out_hbm,
    out_ref,
    x_ref,
    conv_a,
    conv_b,
    time_w,
    time_parts,
    weights,
    padded,
    hidden_ref,
    normed,
    keys_ref,
    values_ref,
    second_ref,
    send_blocks,
    recv_blocks,
    back_blocks,
    final_blocks,
    local_sem,
    time_send,
    time_recv,
    chain_send,
    chain_recv,
    pair_send,
    pair_recv,
    near_send,
    near_recv,
    far_send,
    far_recv,
    relay_send,
    relay_recv,
    go_send,
    go_recv,
    ret_send,
    ret_recv,
):
    tokens, channels = x_ref.shape
    head_width = channels // HEADS
    frame = lax.axis_index("frame")
    video = lax.axis_index("video")
    core = lax.rem(video, 2)
    column = video // 2
    columns = videos // 2
    partner = column * 2 + (1 - core)
    last = frames - 1

    def video_at(shift, which):
        return lax.rem(column + shift, columns) * 2 + which

    barrier = pltpu.get_barrier_semaphore()
    for d in range(1, frames):
        pl.semaphore_signal(
            barrier, inc=1, device_id={"frame": lax.rem(frame + d, frames)}, device_id_type=MESH
        )
    pl.semaphore_signal(barrier, inc=1, device_id={"video": partner}, device_id_type=MESH)
    for d in range(1, columns):
        pl.semaphore_signal(
            barrier, inc=1, device_id={"video": video_at(d, core)}, device_id_type=MESH
        )

    local = [
        (time_hbm, time_w),
        (epi_in_hbm, weights.at[0, frame, pl.ds(0, 3)]),
        (epi_out_hbm, weights.at[0, frame, 3]),
        (x_hbm.at[0, 0], x_ref),
        (conv_a_hbm, conv_a),
        (conv_b_hbm, conv_b),
        (temp_in_hbm, weights.at[1, frame, pl.ds(0, 3)]),
        (temp_out_hbm, weights.at[1, frame, 3]),
    ]
    local = [pltpu.make_async_copy(a, b, local_sem.at[i]) for i, (a, b) in enumerate(local)]
    for copy in local:
        copy.start()
    pl.semaphore_wait(barrier, frames + columns - 1)

    def remote(src, dst, send, recv, **where):
        return pltpu.make_async_remote_copy(
            src_ref=src,
            dst_ref=dst,
            send_sem=send,
            recv_sem=recv,
            device_id=where,
            device_id_type=MESH,
        )

    mine = pl.ds(core * 2, 2)

    def owner(direction, k):
        return frame - k if direction == 0 else frame + k

    def has(direction, k):
        return frame >= k if direction == 0 else frame + k <= last

    def can_pass(direction):
        return frame < last if direction == 0 else frame > 0

    def chain_copy(s, direction, k):
        block = weights.at[s, owner(direction, k), mine]
        to = frame + 1 if direction == 0 else frame - 1
        return remote(
            block, block, chain_send.at[s, direction, k], chain_recv.at[s, direction, k], frame=to
        )

    def pair_copy(s, direction, k):
        block = weights.at[s, owner(direction, k), mine]
        return remote(
            block, block, pair_send.at[s, direction, k], pair_recv.at[s, direction, k], video=partner
        )

    def chain_step(s, k):
        for direction in range(2):
            if k > 0:

                @pl.when(has(direction, k))
                def _():
                    chain_copy_recv(s, direction, k - 1)
                    pair_copy(s, direction, k).start()

            if k < last:

                @pl.when(jnp.logical_and(has(direction, k), can_pass(direction)))
                def _():
                    chain_copy(s, direction, k).start()

    def chain_copy_recv(s, direction, k):
        block = weights.at[s, owner(direction, k + 1), mine]
        remote(
            block, block, chain_send.at[s, direction, k], chain_recv.at[s, direction, k], frame=frame
        ).wait_recv()

    def chain_finish(s):
        other = pl.ds((1 - core) * 2, 2)
        for direction in range(2):
            for k in range(1, frames):

                @pl.when(has(direction, k))
                def _():
                    block = weights.at[s, owner(direction, k), other]
                    remote(
                        block,
                        block,
                        pair_send.at[s, direction, k],
                        pair_recv.at[s, direction, k],
                        video=partner,
                    ).wait_recv()

    def chain_drain(s):
        for direction in range(2):
            for k in range(frames):
                if k > 0:

                    @pl.when(has(direction, k))
                    def _():
                        pair_copy(s, direction, k).wait_send()

                if k < last:

                    @pl.when(jnp.logical_and(has(direction, k), can_pass(direction)))
                    def _():
                        chain_copy(s, direction, k).wait_send()

    def matrix(s, index):
        return jnp.concatenate([weights[s, f, index] for f in range(frames)], axis=0)

    local[0].wait()
    rows = time_w.shape[0]
    place = iota((16, rows), 1) + frame * rows
    is_sin = place >= TEMB // 2
    index = jnp.where(is_sin, place - TEMB // 2, place).astype(F32)
    frequency = jnp.exp(-math.log(10000.0) * index / (TEMB // 2))
    angle = frequency * steps_ref[0].astype(F32)
    basis = wave(angle, jnp.where(is_sin, 3.0, 0.0))
    time_act = (basis * (1.0 / (1.0 + jnp.exp(-basis)))).astype(BF16)
    time_parts[0] = dot(time_act, time_w[...])[0:8]

    def time_copy(d):
        return remote(
            time_parts.at[0],
            time_parts.at[d],
            time_send.at[d - 1],
            time_recv.at[d - 1],
            frame=lax.rem(frame + d, frames),
        )

    for d in range(1, frames):
        time_copy(d).start()
    local[1].wait()
    local[2].wait()
    chain_step(0, 0)

    group_width = channels // NORM_GROUPS
    row_group = jnp.floor((iota((channels, channels), 0).astype(F32) + 0.5) / group_width)
    col_group = jnp.floor((iota((channels, channels), 1).astype(F32) + 0.5) / group_width)
    same_group = jnp.where(row_group == col_group, 1.0, 0.0).astype(BF16)
    count = float(tokens * group_width)
    spot = jnp.bitwise_and(iota((tokens, channels), 0), W - 1)
    border = jnp.zeros((W, channels), BF16)
    for side in range(3):
        padded[side, 0:W] = border
        padded[side, W + tokens : W + tokens + W] = border

    def spread_act(act):
        padded[1, W : W + tokens] = act.astype(BF16)
        before = jnp.where(spot == 0, 0.0, pltpu.roll(act, 1, 0))
        padded[0, W : W + tokens] = before.astype(BF16)
        after = jnp.where(spot == W - 1, 0.0, pltpu.roll(act, tokens - 1, 0))
        padded[2, W : W + tokens] = after.astype(BF16)

    def convolve(weight, start, size):
        total = None
        for a in range(3):
            for b in range(3):
                term = dot(padded[b, start + W * a : start + W * a + size], weight[a, b])
                total = term if total is None else total + term
        return total

    local[3].wait()
    spread_act(gn_silu(x_ref[...].astype(F32), same_group, count))
    local[4].wait()
    inner = convolve(conv_a, 0, tokens)
    chain_step(0, 1)
    bias = time_parts[0, 0:1]
    for d in range(1, frames):
        time_copy(d).wait_recv()
        bias = bias + time_parts[d, 0:1]
    spread_act(gn_silu(inner + bias, same_group, count))
    local[5].wait()
    local[6].wait()
    local[7].wait()
    half = tokens // 2

    def near_copy(c):
        block = normed.at[video, c]
        return remote(block, block, near_send.at[c], near_recv.at[c], video=partner)

    def far_copy(d, c):
        block = normed.at[video, c]
        return remote(
            block, block, far_send.at[d - 1, c], far_recv.at[d - 1, c], video=video_at(d, core)
        )

    def relay_copy(d, c):
        block = normed.at[video_at(columns - d, core), c]
        return remote(
            block, block, relay_send.at[d - 1, c], relay_recv.at[d - 1, c], video=partner
        )

    for c in range(2):
        part = slice(c * half, (c + 1) * half)
        hidden = (x_ref[part].astype(F32) + convolve(conv_b, c * half, half)).astype(BF16)
        hidden_ref[part] = hidden
        normed[video, c] = layer_norm(hidden.astype(F32)).astype(BF16)
        for d in range(1, columns):
            far_copy(d, c).start()
        near_copy(c).start()
        if c == 0:
            chain_step(0, 2)
    for k in range(3, frames):
        chain_step(0, k)
    chain_step(1, 0)
    chain_finish(0)

    w_query, w_key, w_value = matrix(0, 0), matrix(0, 1), matrix(0, 2)

    def project(u):
        both = normed[u].reshape(tokens, channels)
        keys_ref[u] = dot(both, w_key).astype(BF16)
        values_ref[u] = dot(both, w_value).astype(BF16)

    queries = dot(normed[video].reshape(tokens, channels), w_query).astype(BF16)
    project(video)
    for d in range(1, columns):
        for c in range(2):
            block = normed.at[video_at(columns - d, core), c]
            remote(
                block, block, far_send.at[d - 1, c], far_recv.at[d - 1, c], video=video
            ).wait_recv()
            relay_copy(d, c).start()
        if d == 1:
            for c in range(2):
                block = normed.at[partner, c]
                remote(block, block, near_send.at[c], near_recv.at[c], video=partner).wait_recv()
            project(partner)
        project(video_at(columns - d, core))
    chain_step(1, 1)
    for d in range(1, columns):
        for c in range(2):
            block = normed.at[video_at(columns - d, 1 - core), c]
            remote(
                block, block, relay_send.at[d - 1, c], relay_recv.at[d - 1, c], video=partner
            ).wait_recv()
        project(video_at(columns - d, 1 - core))

    exponent = math.log2(math.e) / math.sqrt(head_width)
    w_out = matrix(0, 3)
    lane_row = iota((1, tokens), 1)
    ones = jnp.ones((tokens, 128), BF16)
    rows_per = tokens // chunks // frames

    def go_copy(c, d):
        to = lax.rem(frame + d, frames)
        return remote(
            send_blocks.at[c, to],
            recv_blocks.at[c, frame],
            go_send.at[c, d - 1],
            go_recv.at[c, d - 1],
            frame=to,
        )

    def ret_copy(c, d):
        to = lax.rem(frame + d, frames)
        return remote(
            back_blocks.at[c, to],
            final_blocks.at[c, frame],
            ret_send.at[c, d - 1],
            ret_recv.at[c, d - 1],
            frame=to,
        )

    def attend(i):
        part = slice(i * half, (i + 1) * half)
        blocks = [jnp.zeros((half, min(128, channels - s)), F32) for s in range(0, channels, 128)]
        for m in range(2):
            target = match_ref[m, video]
            keys = keys_ref[target]
            values = values_ref[target]
            bias_low = jnp.where(mask_ref[m, video, i, 0] > 0, 0.0, FILL)
            bias_high = jnp.where(mask_ref[m, video, i, 1] > 0, 0.0, FILL)
            bias_row = jnp.where(lane_row < half, bias_low, bias_high)
            for h in range(HEADS):
                low = h * head_width // 128 * 128
                high = min(-(-(h + 1) * head_width // 128) * 128, channels)
                lanes = iota((1, high - low), 1) + low
                inside = jnp.logical_and(lanes >= h * head_width, lanes < (h + 1) * head_width)
                inside = jnp.where(inside, 1.0, 0.0).astype(BF16)
                scores = dot_nt(queries[part, low:high] * inside, keys[:, low:high]) + bias_row
                peak = jnp.max(scores, axis=-1, keepdims=True)
                powers = jnp.exp2((scores - peak) * exponent).astype(BF16)
                total = 1.0 / dot(powers, ones)
                result = dot(powers, values[:, low:high] * inside)
                for s in range(low, high, 128):
                    width = min(128, channels - s)
                    blocks[s // 128] = (
                        blocks[s // 128]
                        + result[:, s - low : s - low + width] * total[:, :width]
                    )
        mixture = jnp.concatenate(blocks, axis=1).astype(BF16)
        second = (hidden_ref[part].astype(F32) + dot(mixture, w_out)).astype(BF16)
        second_ref[part] = second
        return layer_norm(second.astype(F32)).astype(BF16)

    def send_out(c, temp_normed):
        send_blocks[c] = temp_normed.reshape(frames, rows_per, channels)
        for d in range(1, frames):
            go_copy(c, d).start()
        recv_blocks[c, frame] = send_blocks[c, frame]

    if chunks == 2:
        send_out(0, attend(0))
        chain_step(1, 2)
        send_out(1, attend(1))
    else:
        first = attend(0)
        chain_step(1, 2)
        second_part = attend(1)
        send_out(0, jnp.concatenate([first, second_part], axis=0))
    for k in range(3, frames):
        chain_step(1, k)
    chain_finish(1)

    w_tq, w_tk, w_tv = matrix(1, 0), matrix(1, 1), matrix(1, 2)
    w_tout = matrix(1, 3)
    lane_head = jnp.floor((iota((channels, 128), 0).astype(F32) + 0.5) / head_width)
    gather_heads = jnp.where(
        lane_head == iota((channels, 128), 1).astype(F32), 1.0, 0.0
    ).astype(BF16)
    row_head = jnp.floor((iota((128, channels), 1).astype(F32) + 0.5) / head_width)
    spread_heads = jnp.where(
        row_head == iota((128, channels), 0).astype(F32), 1.0, 0.0
    ).astype(BF16)

    for c in range(chunks):
        for d in range(1, frames):
            block = recv_blocks.at[c, lax.rem(frame + frames - d, frames)]
            remote(
                block, block, go_send.at[c, d - 1], go_recv.at[c, d - 1], frame=frame
            ).wait_recv()
        stacked = recv_blocks[c].reshape(frames * rows_per, channels)
        q = dot(stacked, w_tq).astype(BF16).astype(F32)
        k = dot(stacked, w_tk).astype(BF16).astype(F32)
        v = dot(stacked, w_tv).astype(BF16).astype(F32)
        for f in range(frames):
            q_f = q[f * rows_per : (f + 1) * rows_per]
            product = jnp.concatenate([q_f] * frames, axis=0) * k
            coarse = product.astype(BF16)
            fine = (product - coarse.astype(F32)).astype(BF16)
            scores = dot(coarse, gather_heads) + dot(fine, gather_heads)
            parts = [scores[g * rows_per : (g + 1) * rows_per] for g in range(frames)]
            peak = functools.reduce(jnp.maximum, parts)
            parts = [jnp.exp2((p - peak) * exponent) for p in parts]
            scale = 1.0 / functools.reduce(jnp.add, parts)
            probs = jnp.concatenate([p * scale for p in parts], axis=0).astype(BF16)
            weighted = dot(probs, spread_heads) * v
            summed = functools.reduce(
                jnp.add, [weighted[g * rows_per : (g + 1) * rows_per] for g in range(frames)]
            )
            back_blocks[c, f] = summed.astype(BF16)
        for d in range(1, frames):
            ret_copy(c, d).start()
        final_blocks[c, frame] = back_blocks[c, frame]

    span = tokens // chunks
    for c in range(chunks):
        for d in range(1, frames):
            block = final_blocks.at[c, lax.rem(frame + frames - d, frames)]
            remote(
                block, block, ret_send.at[c, d - 1], ret_recv.at[c, d - 1], frame=frame
            ).wait_recv()
        part = slice(c * span, (c + 1) * span)
        outcome = final_blocks[c].reshape(span, channels)
        out_ref[0, 0, part] = (second_ref[part].astype(F32) + dot(outcome, w_tout)).astype(BF16)

    for d in range(1, frames):
        time_copy(d).wait_send()
        for c in range(chunks):
            go_copy(c, d).wait_send()
            ret_copy(c, d).wait_send()
    for c in range(2):
        near_copy(c).wait_send()
        for d in range(1, columns):
            far_copy(d, c).wait_send()
            relay_copy(d, c).wait_send()
    chain_drain(0)
    chain_drain(1)


def per_device(frames, videos, *args):
    (
        latents,
        timesteps,
        matchings,
        tile_mask,
        conv_first,
        conv_second,
        time_proj,
        epi_in,
        epi_out,
        temp_in,
        temp_out,
    ) = args
    tokens, channels = latents.shape[2:]
    rows = epi_out.shape[0]
    columns = videos // 2
    chunks = 2 if (tokens // 2 // frames) % 16 == 0 else 1
    block = (chunks, frames, tokens // chunks // frames, channels)
    dma = pltpu.SemaphoreType.DMA
    hops = max(columns - 1, 1)
    anywhere = pl.BlockSpec(memory_space=pl.ANY)
    scalar = pl.BlockSpec(memory_space=pltpu.SMEM)
    return pl.pallas_call(
        functools.partial(kernel, frames, videos, chunks),
        out_shape=jax.ShapeDtypeStruct(latents.shape, BF16),
        in_specs=[scalar] * 3 + [anywhere] * 8,
        out_specs=pl.BlockSpec(memory_space=pltpu.VMEM),
        scratch_shapes=[
            pltpu.VMEM((tokens, channels), BF16),
            pltpu.VMEM(conv_first.shape, BF16),
            pltpu.VMEM(conv_second.shape, BF16),
            pltpu.VMEM(time_proj.shape, BF16),
            pltpu.VMEM((frames, 8, channels), F32),
            pltpu.VMEM((2, frames, 4, rows, channels), BF16),
            pltpu.VMEM((3, tokens + 2 * W, channels), BF16),
            pltpu.VMEM((tokens, channels), BF16),
            pltpu.VMEM((videos, 2, tokens // 2, channels), BF16),
            pltpu.VMEM((videos, tokens, channels), BF16),
            pltpu.VMEM((videos, tokens, channels), BF16),
            pltpu.VMEM((tokens, channels), BF16),
            pltpu.VMEM(block, BF16),
            pltpu.VMEM(block, BF16),
            pltpu.VMEM(block, BF16),
            pltpu.VMEM(block, BF16),
            dma((8,)),
            dma((frames,)),
            dma((frames,)),
            dma((2, 2, frames)),
            dma((2, 2, frames)),
            dma((2, 2, frames)),
            dma((2, 2, frames)),
            dma((2,)),
            dma((2,)),
            dma((hops, 2)),
            dma((hops, 2)),
            dma((hops, 2)),
            dma((hops, 2)),
            dma((chunks, frames)),
            dma((chunks, frames)),
            dma((chunks, frames)),
            dma((chunks, frames)),
        ],
        compiler_params=pltpu.CompilerParams(collective_id=0, has_side_effects=True),
    )(
        timesteps,
        matchings,
        tile_mask,
        latents,
        conv_first,
        conv_second,
        time_proj,
        epi_in,
        epi_out,
        temp_in,
        temp_out,
    )


def solution(mesh):
    placed = (
        P(("groups", "video"), "frame", None, None),
        P(("groups", "video")),
        P(None, "groups"),
        P(None, "groups", None, None),
        P(),
        P(),
        P("frame", None),
        P(None, "frame", None),
        P("frame", None),
        P(None, "frame", None),
        P("frame", None),
    )
    return jax.shard_map(
        functools.partial(per_device, mesh.shape["frame"], mesh.shape["video"]),
        mesh=mesh,
        in_specs=placed,
        out_specs=P(("groups", "video"), "frame", None, None),
        check_vma=False,
    )
```

time: 145 us -> 48.2 us (0.33)
  blocking collectives: 98.7 us -> 0 us
  Pallas kernels: 0 us -> 42.5 us
  matrix products: 22.1 us -> 0 us
  starting transfers between devices: 6.73 us -> 0 us
  local copies, waits for them, and re-layouts: 10.5 us -> 4.82 us
  other arithmetic: 4.76 us -> 0 us
    all_gather x6 -> x0, blocking collectives: 98.7 us -> none  [the longest x1 23.7 us: per_device(): lax.all_gather(time_proj, 'frame', axis=0, tiled=True)]
    pallas_call x0 -> x1, Pallas kernels: none -> 42.5 us  [per_device(): pl.pallas_call(functools.partial(kernel, frames, videos, chunks), out_sha...]
    dot_general x31 -> x0, matrix products: 15 us -> none  [the longest x18 6.75 us: convolve(): jnp.dot(window, weight[row_shift, col_shift], preferred_element_type=jnp....]
    sub x3 -> x0, matrix products: 7.07 us -> none  [softmax_last(): powers = jnp.exp(scores - maxima)]
    all_to_all x2 -> x0, starting transfers between devices: 6.73 us -> none  [the longest x1 3.36 us: per_device(): lax.all_to_all(attended, 'frame', split_axis=0, concat_axis=0, tiled=True)]
    convert_element_type x8 -> x0, local copies, waits for them, and re-layouts: 4.19 us -> none  [the longest x1 1.94 us: per_device(): source.astype(jnp.float32) + convolve(second_act, conv_second)]
    reshape x4 -> x0, local copies, waits for them, and re-layouts: 3.19 us -> none  [the longest x1 0.84 us: frame_attention(): return result.astype(jnp.bfloat16).reshape(frames, pixels, channels)]
    reduce_sum x9 -> x0, other arithmetic: 3.02 us -> none  [the longest x4 1.59 us: group_norm(): spread = jnp.mean(jnp.square(grouped - average), axis=(0, 2), keepdims=True)]
  transfers between devices with their start and end apart: 2 -> 0, of which waited for: 0 -> 0; matrix products, arithmetic and copies ran while one was open for 0% -> 0% of each run, Pallas kernels for 0% -> 0%
where the time goes in v1:
time: 48.2 us; the launch traced here: 48 us
  Pallas kernels  42.5 us (88%)
  local copies, waits for them, and re-layouts  4.82 us (10%)
  between operations  0.66 us (1%)
    pallas_call x1, Pallas kernels, per_device(): pl.pallas_call(functools.partial(kernel, frames, videos, chunks), out_sha...  42.5 us
    unnamed x2, local copies, waits for them, and re-layouts  3.11 us
    pallas_call x1, local copies, waits for them, and re-layouts, per_device(): pl.pallas_call(functools.partial(kernel, frames, videos, chunks), out_sha...  1.71 us

profile of v1, /device:TPU:0, one launch (start us, length us, event | category | flops | bytes accessed | tf_op | source)
XLA Modules:
  0.0 48.0 jit_solution(3970212104939868785)
XLA Ops:
  0.7 1.4 %copy.12.mask_ref = s32[2,4,2,2]{3,2,1,0:T(2,128)} copy(s32[2,4,2,2]{1,3,2,0:T(2,128)} %param.14) | data formatting | bytes 256 | tf_op args[3]
  2.0 1.7 %copy.13.x_hbm = bf16[1,1,256,320]{3,2,1,0:T(8,128)(2,1)} copy(bf16[1,1,256,320]{2,3,1,0:T(8,128)(2,1)} %param.11) | data formatting | bytes 327680 | tf_op args[0]
  3.8 42.5 %shard_map.109 = bf16[1,1,256,320]{3,2,1,0:T(8,128)(2,1)} custom-call(s32[1]{0:T(128)S(6)} %copy.15.steps_ref, s32[2,4]{1,0:T(2,128)} %match_ref.1, s32[2,4,2,2]{3,2,1,0:T(2,128)} %copy.12.mask_ref, bf16[1,1,256,320]{3,2,1,0:T(8,128)(2,1)} %copy.13.x_hbm, bf16[3,3,320,320]{3,2,1,0:T(8,128)(2,1)} %conv_a_hbm.1, bf16[3,3,320,320]{3,2,1,0:T(8,128)(2,1)} %conv_b_hbm.1, ...), custom_call_target="tpu_custom_call" | custom-call | tf_op jit(solution)/shard_map/pallas_call | solution.py:558
  46.3 1.7 %copy.14 = bf16[1,1,256,320]{2,3,1,0:T(8,128)(2,1)} copy(bf16[1,1,256,320]{3,2,1,0:T(8,128)(2,1)} %shard_map.109) | data formatting | bytes 327680 | tf_op jit(solution)/shard_map/pallas_call | solution.py:558

commit v2 on v1

--- a/solution.py
+++ b/solution.py
@@ -98,6 +98,7 @@
     temp_in_hbm,
     temp_out_hbm,
     out_ref,
+    xt_ref,
     x_ref,
     conv_a,
     conv_b,
@@ -132,7 +133,7 @@
     ret_send,
     ret_recv,
 ):
-    tokens, channels = x_ref.shape
+    channels, tokens = xt_ref.shape
     head_width = channels // HEADS
     frame = lax.axis_index("frame")
     video = lax.axis_index("video")
@@ -158,13 +159,17 @@
 
     local = [
         (time_hbm, time_w),
-        (epi_in_hbm, weights.at[0, frame, pl.ds(0, 3)]),
-        (epi_out_hbm, weights.at[0, frame, 3]),
-        (x_hbm.at[0, 0], x_ref),
+        (epi_in_hbm.at[1], weights.at[frame, 0]),
+        (epi_in_hbm.at[2], weights.at[frame, 1]),
+        (x_hbm.at[0, 0], xt_ref),
+        (epi_in_hbm.at[0], weights.at[frame, 2]),
+        (epi_out_hbm, weights.at[frame, 3]),
         (conv_a_hbm, conv_a),
         (conv_b_hbm, conv_b),
-        (temp_in_hbm, weights.at[1, frame, pl.ds(0, 3)]),
-        (temp_out_hbm, weights.at[1, frame, 3]),
+        (temp_in_hbm.at[1], weights.at[frame, 4]),
+        (temp_in_hbm.at[2], weights.at[frame, 5]),
+        (temp_in_hbm.at[0], weights.at[frame, 6]),
+        (temp_out_hbm, weights.at[frame, 7]),
     ]
     local = [pltpu.make_async_copy(a, b, local_sem.at[i]) for i, (a, b) in enumerate(local)]
     for copy in local:
@@ -181,7 +186,6 @@
             device_id_type=MESH,
         )
 
-    mine = pl.ds(core * 2, 2)
 
     def owner(direction, k):
         return frame - k if direction == 0 else frame + k
@@ -193,14 +197,14 @@
         return frame < last if direction == 0 else frame > 0
 
     def chain_copy(s, direction, k):
-        block = weights.at[s, owner(direction, k), mine]
+        block = weights.at[owner(direction, k), s * 2 + core]
         to = frame + 1 if direction == 0 else frame - 1
         return remote(
             block, block, chain_send.at[s, direction, k], chain_recv.at[s, direction, k], frame=to
         )
 
     def pair_copy(s, direction, k):
-        block = weights.at[s, owner(direction, k), mine]
+        block = weights.at[owner(direction, k), s * 2 + core]
         return remote(
             block, block, pair_send.at[s, direction, k], pair_recv.at[s, direction, k], video=partner
         )
@@ -221,19 +225,18 @@
                     chain_copy(s, direction, k).start()
 
     def chain_copy_recv(s, direction, k):
-        block = weights.at[s, owner(direction, k + 1), mine]
+        block = weights.at[owner(direction, k + 1), s * 2 + core]
         remote(
             block, block, chain_send.at[s, direction, k], chain_recv.at[s, direction, k], frame=frame
         ).wait_recv()
 
     def chain_finish(s):
-        other = pl.ds((1 - core) * 2, 2)
         for direction in range(2):
             for k in range(1, frames):
 
                 @pl.when(has(direction, k))
                 def _():
-                    block = weights.at[s, owner(direction, k), other]
+                    block = weights.at[owner(direction, k), s * 2 + 1 - core]
                     remote(
                         block,
                         block,
@@ -257,8 +260,8 @@
                     def _():
                         chain_copy(s, direction, k).wait_send()
 
-    def matrix(s, index):
-        return jnp.concatenate([weights[s, f, index] for f in range(frames)], axis=0)
+    def matrix(index):
+        return jnp.concatenate([weights[f, index] for f in range(frames)], axis=0)
 
     local[0].wait()
     rows = time_w.shape[0]
@@ -285,6 +288,9 @@
     local[1].wait()
     local[2].wait()
     chain_step(0, 0)
+    local[4].wait()
+    local[5].wait()
+    chain_step(1, 0)
 
     group_width = channels // NORM_GROUPS
     row_group = jnp.floor((iota((channels, channels), 0).astype(F32) + 0.5) / group_width)
@@ -313,8 +319,10 @@
         return total
 
     local[3].wait()
-    spread_act(gn_silu(x_ref[...].astype(F32), same_group, count))
-    local[4].wait()
+    source = jnp.transpose(xt_ref[...].astype(F32))
+    x_ref[...] = source.astype(BF16)
+    spread_act(gn_silu(source, same_group, count))
+    local[6].wait()
     inner = convolve(conv_a, 0, tokens)
     chain_step(0, 1)
     bias = time_parts[0, 0:1]
@@ -322,8 +330,7 @@
         time_copy(d).wait_recv()
         bias = bias + time_parts[d, 0:1]
     spread_act(gn_silu(inner + bias, same_group, count))
-    local[5].wait()
-    local[6].wait()
+    chain_step(1, 1)
     local[7].wait()
     half = tokens // 2
 
@@ -351,21 +358,22 @@
         for d in range(1, columns):
             far_copy(d, c).start()
         near_copy(c).start()
-        if c == 0:
-            chain_step(0, 2)
-    for k in range(3, frames):
-        chain_step(0, k)
-    chain_step(1, 0)
+        chain_step(c, 2)
+    for copy in local[8:]:
+        copy.wait()
+    for s in range(2):
+        for k in range(3, frames):
+            chain_step(s, k)
+        chain_step(s + 2, 0)
     chain_finish(0)
 
-    w_query, w_key, w_value = matrix(0, 0), matrix(0, 1), matrix(0, 2)
+    w_key, w_value = matrix(0), matrix(1)
 
     def project(u):
         both = normed[u].reshape(tokens, channels)
         keys_ref[u] = dot(both, w_key).astype(BF16)
         values_ref[u] = dot(both, w_value).astype(BF16)
 
-    queries = dot(normed[video].reshape(tokens, channels), w_query).astype(BF16)
     project(video)
     for d in range(1, columns):
         for c in range(2):
@@ -380,7 +388,10 @@
                 remote(block, block, near_send.at[c], near_recv.at[c], video=partner).wait_recv()
             project(partner)
         project(video_at(columns - d, core))
-    chain_step(1, 1)
+    chain_step(2, 1)
+    chain_finish(1)
+    queries = dot(normed[video].reshape(tokens, channels), matrix(2)).astype(BF16)
+    chain_step(3, 1)
     for d in range(1, columns):
         for c in range(2):
             block = normed.at[video_at(columns - d, 1 - core), c]
@@ -390,7 +401,7 @@
         project(video_at(columns - d, 1 - core))
 
     exponent = math.log2(math.e) / math.sqrt(head_width)
-    w_out = matrix(0, 3)
+    w_out = matrix(3)
     lane_row = iota((1, tokens), 1)
     ones = jnp.ones((tokens, 128), BF16)
     rows_per = tokens // chunks // frames
@@ -422,8 +433,8 @@
             target = match_ref[m, video]
             keys = keys_ref[target]
             values = values_ref[target]
-            bias_low = jnp.where(mask_ref[m, video, i, 0] > 0, 0.0, FILL)
-            bias_high = jnp.where(mask_ref[m, video, i, 1] > 0, 0.0, FILL)
+            bias_low = jnp.where(mask_ref[m, i, 0, video] > 0, 0.0, FILL)
+            bias_high = jnp.where(mask_ref[m, i, 1, video] > 0, 0.0, FILL)
             bias_row = jnp.where(lane_row < half, bias_low, bias_high)
             for h in range(HEADS):
                 low = h * head_width // 128 * 128
@@ -455,19 +466,22 @@
 
     if chunks == 2:
         send_out(0, attend(0))
-        chain_step(1, 2)
+        chain_step(2, 2)
+        chain_step(3, 2)
         send_out(1, attend(1))
     else:
         first = attend(0)
-        chain_step(1, 2)
+        chain_step(2, 2)
+        chain_step(3, 2)
         second_part = attend(1)
         send_out(0, jnp.concatenate([first, second_part], axis=0))
-    for k in range(3, frames):
-        chain_step(1, k)
-    chain_finish(1)
-
-    w_tq, w_tk, w_tv = matrix(1, 0), matrix(1, 1), matrix(1, 2)
-    w_tout = matrix(1, 3)
+    for s in range(2, 4):
+        for k in range(3, frames):
+            chain_step(s, k)
+    chain_finish(2)
+    chain_finish(3)
+
+    w_tk, w_tv, w_tq, w_tout = matrix(4), matrix(5), matrix(6), matrix(7)
     lane_head = jnp.floor((iota((channels, 128), 0).astype(F32) + 0.5) / head_width)
     gather_heads = jnp.where(
         lane_head == iota((channels, 128), 1).astype(F32), 1.0, 0.0
@@ -516,7 +530,8 @@
             ).wait_recv()
         part = slice(c * span, (c + 1) * span)
         outcome = final_blocks[c].reshape(span, channels)
-        out_ref[0, 0, part] = (second_ref[part].astype(F32) + dot(outcome, w_tout)).astype(BF16)
+        result = second_ref[part].astype(F32) + dot(outcome, w_tout)
+        out_ref[0, 0, :, part] = jnp.transpose(result).astype(BF16)
 
     for d in range(1, frames):
         time_copy(d).wait_send()
@@ -528,8 +543,8 @@
         for d in range(1, columns):
             far_copy(d, c).wait_send()
             relay_copy(d, c).wait_send()
-    chain_drain(0)
-    chain_drain(1)
+    for s in range(4):
+        chain_drain(s)
 
 
 def per_device(frames, videos, *args):
@@ -555,18 +570,19 @@
     hops = max(columns - 1, 1)
     anywhere = pl.BlockSpec(memory_space=pl.ANY)
     scalar = pl.BlockSpec(memory_space=pltpu.SMEM)
-    return pl.pallas_call(
+    result = pl.pallas_call(
         functools.partial(kernel, frames, videos, chunks),
-        out_shape=jax.ShapeDtypeStruct(latents.shape, BF16),
+        out_shape=jax.ShapeDtypeStruct((1, 1, channels, tokens), BF16),
         in_specs=[scalar] * 3 + [anywhere] * 8,
         out_specs=pl.BlockSpec(memory_space=pltpu.VMEM),
         scratch_shapes=[
+            pltpu.VMEM((channels, tokens), BF16),
             pltpu.VMEM((tokens, channels), BF16),
             pltpu.VMEM(conv_first.shape, BF16),
             pltpu.VMEM(conv_second.shape, BF16),
             pltpu.VMEM(time_proj.shape, BF16),
             pltpu.VMEM((frames, 8, channels), F32),
-            pltpu.VMEM((2, frames, 4, rows, channels), BF16),
+            pltpu.VMEM((frames, 8, rows, channels), BF16),
             pltpu.VMEM((3, tokens + 2 * W, channels), BF16),
             pltpu.VMEM((tokens, channels), BF16),
             pltpu.VMEM((videos, 2, tokens // 2, channels), BF16),
@@ -577,13 +593,13 @@
             pltpu.VMEM(block, BF16),
             pltpu.VMEM(block, BF16),
             pltpu.VMEM(block, BF16),
-            dma((8,)),
+            dma((12,)),
             dma((frames,)),
             dma((frames,)),
-            dma((2, 2, frames)),
-            dma((2, 2, frames)),
-            dma((2, 2, frames)),
-            dma((2, 2, frames)),
+            dma((4, 2, frames)),
+            dma((4, 2, frames)),
+            dma((4, 2, frames)),
+            dma((4, 2, frames)),
             dma((2,)),
             dma((2,)),
             dma((hops, 2)),
@@ -599,8 +615,8 @@
     )(
         timesteps,
         matchings,
-        tile_mask,
-        latents,
+        jnp.transpose(tile_mask, (0, 2, 3, 1)),
+        jnp.swapaxes(latents, 2, 3),
         conv_first,
         conv_second,
         time_proj,
@@ -609,6 +625,7 @@
         temp_in,
         temp_out,
     )
+    return jnp.swapaxes(result, 2, 3)
 
 
 def solution(mesh):

time: 48.2 us -> 44.2 us (0.917)
  local copies, waits for them, and re-layouts: 4.82 us -> 1.59 us
  Pallas kernels: 42.5 us -> 41.8 us
    pallas_call x1 -> x0, local copies, waits for them, and re-layouts: 1.71 us -> none  [per_device(): pl.pallas_call(functools.partial(kernel, frames, videos, chunks), out_sha...]
    unnamed x2 -> x1, local copies, waits for them, and re-layouts: 3.11 us -> 1.59 us
    pallas_call x1, Pallas kernels: 42.5 us -> 41.8 us  [per_device(): pl.pallas_call(functools.partial(kernel, frames, videos, chunks), out_sha...]
where the time goes in v2:
time: 44.2 us; the launch traced here: 44 us
  Pallas kernels  41.8 us (95%)
  local copies, waits for them, and re-layouts  1.59 us (4%)
  between operations  0.66 us (1%)
    pallas_call x1, Pallas kernels, per_device(): pl.pallas_call(functools.partial(kernel, frames, videos, chunks), out_sha...  41.8 us
    unnamed x1, local copies, waits for them, and re-layouts  1.59 us

profile of v2, /device:TPU:0, one launch (start us, length us, event | category | flops | bytes accessed | tf_op | source)
XLA Modules:
  0.0 44.0 jit_solution(17010192310235785528)
XLA Ops:
  0.7 41.8 %shard_map.109 = bf16[1,1,320,256]{3,2,1,0:T(8,128)(2,1)} custom-call(s32[1]{0:T(128)S(6)} %copy.13.steps_ref, s32[2,4]{1,0:T(2,128)} %match_ref.1, s32[2,2,2,4]{3,2,1,0:T(2,128)} %bitcast.5, bf16[1,1,320,256]{3,2,1,0:T(8,128)(2,1)} %bitcast.4, bf16[3,3,320,320]{3,2,1,0:T(8,128)(2,1)} %conv_a_hbm.1, bf16[3,3,320,320]{3,2,1,0:T(8,128)(2,1)} %conv_b_hbm.1, ...), custom_call_target="tpu_custom_call" | custom-call | tf_op jit(solution)/shard_map/pallas_call | solution.py:573
  42.4 1.6 %copy.14 = bf16[1,1,256,320]{2,3,1,0:T(8,128)(2,1)} copy(bf16[1,1,256,320]{2,3,1,0:T(8,128)(2,1)} %bitcast.3) | data formatting | bytes 327680

commit v3 on v2

--- a/solution.py
+++ b/solution.py
@@ -86,9 +86,9 @@
     frames,
     videos,
     chunks,
-    steps_ref,
-    match_ref,
-    mask_ref,
+    steps_hbm,
+    match_hbm,
+    mask_hbm,
     x_hbm,
     conv_a_hbm,
     conv_b_hbm,
@@ -98,6 +98,9 @@
     temp_in_hbm,
     temp_out_hbm,
     out_ref,
+    steps_ref,
+    match_ref,
+    mask_ref,
     xt_ref,
     x_ref,
     conv_a,
@@ -170,11 +173,13 @@
         (temp_in_hbm.at[2], weights.at[frame, 5]),
         (temp_in_hbm.at[0], weights.at[frame, 6]),
         (temp_out_hbm, weights.at[frame, 7]),
+        (steps_hbm, steps_ref),
+        (match_hbm, match_ref),
+        (mask_hbm, mask_ref),
     ]
     local = [pltpu.make_async_copy(a, b, local_sem.at[i]) for i, (a, b) in enumerate(local)]
-    for copy in local:
-        copy.start()
-    pl.semaphore_wait(barrier, frames + columns - 1)
+    for i in (12, 0, 3, 1, 2, 4, 5, 6, 7, 8, 9, 10, 11, 13, 14):
+        local[i].start()
 
     def remote(src, dst, send, recv, **where):
         return pltpu.make_async_remote_copy(
@@ -263,6 +268,7 @@
     def matrix(index):
         return jnp.concatenate([weights[f, index] for f in range(frames)], axis=0)
 
+    local[12].wait()
     local[0].wait()
     rows = time_w.shape[0]
     place = iota((16, rows), 1) + frame * rows
@@ -283,14 +289,6 @@
             frame=lax.rem(frame + d, frames),
         )
 
-    for d in range(1, frames):
-        time_copy(d).start()
-    local[1].wait()
-    local[2].wait()
-    chain_step(0, 0)
-    local[4].wait()
-    local[5].wait()
-    chain_step(1, 0)
 
     group_width = channels // NORM_GROUPS
     row_group = jnp.floor((iota((channels, channels), 0).astype(F32) + 0.5) / group_width)
@@ -322,6 +320,13 @@
     source = jnp.transpose(xt_ref[...].astype(F32))
     x_ref[...] = source.astype(BF16)
     spread_act(gn_silu(source, same_group, count))
+    for i in (1, 2, 4, 5):
+        local[i].wait()
+    pl.semaphore_wait(barrier, frames + columns - 1)
+    for d in range(1, frames):
+        time_copy(d).start()
+    chain_step(0, 0)
+    chain_step(1, 0)
     local[6].wait()
     inner = convolve(conv_a, 0, tokens)
     chain_step(0, 1)
@@ -358,9 +363,10 @@
         for d in range(1, columns):
             far_copy(d, c).start()
         near_copy(c).start()
-        chain_step(c, 2)
-    for copy in local[8:]:
-        copy.wait()
+    chain_step(0, 2)
+    chain_step(1, 2)
+    for i in (8, 9, 10, 11, 13, 14):
+        local[i].wait()
     for s in range(2):
         for k in range(3, frames):
             chain_step(s, k)
@@ -445,8 +451,13 @@
                 scores = dot_nt(queries[part, low:high] * inside, keys[:, low:high]) + bias_row
                 peak = jnp.max(scores, axis=-1, keepdims=True)
                 powers = jnp.exp2((scores - peak) * exponent).astype(BF16)
-                total = 1.0 / dot(powers, ones)
-                result = dot(powers, values[:, low:high] * inside)
+                picked = values[:, low:high] * inside
+                if high - low == 128:
+                    result = dot(powers, jnp.concatenate([picked, ones], axis=1))
+                    total = 1.0 / result[:, 128:]
+                else:
+                    total = 1.0 / dot(powers, ones)
+                    result = dot(powers, picked)
                 for s in range(low, high, 128):
                     width = min(128, channels - s)
                     blocks[s // 128] = (
@@ -569,13 +580,15 @@
     dma = pltpu.SemaphoreType.DMA
     hops = max(columns - 1, 1)
     anywhere = pl.BlockSpec(memory_space=pl.ANY)
-    scalar = pl.BlockSpec(memory_space=pltpu.SMEM)
     result = pl.pallas_call(
         functools.partial(kernel, frames, videos, chunks),
         out_shape=jax.ShapeDtypeStruct((1, 1, channels, tokens), BF16),
-        in_specs=[scalar] * 3 + [anywhere] * 8,
+        in_specs=[anywhere] * 11,
         out_specs=pl.BlockSpec(memory_space=pltpu.VMEM),
         scratch_shapes=[
+            pltpu.SMEM(timesteps.shape, jnp.int32),
+            pltpu.SMEM(matchings.shape, jnp.int32),
+            pltpu.SMEM((2, 2, 2, tile_mask.shape[1]), jnp.int32),
             pltpu.VMEM((channels, tokens), BF16),
             pltpu.VMEM((tokens, channels), BF16),
             pltpu.VMEM(conv_first.shape, BF16),
@@ -593,7 +606,7 @@
             pltpu.VMEM(block, BF16),
             pltpu.VMEM(block, BF16),
             pltpu.VMEM(block, BF16),
-            dma((12,)),
+            dma((15,)),
             dma((frames,)),
             dma((frames,)),
             dma((4, 2, frames)),

time: 44.2 us -> 42.1 us (0.952)
  Pallas kernels: 41.8 us -> 39.7 us
    pallas_call x1, Pallas kernels: 41.8 us -> 39.7 us  [per_device(): pl.pallas_call(functools.partial(kernel, frames, videos, chunks), out_sha...]
where the time goes in v3:
time: 42.1 us; the launch traced here: 41.9 us
  Pallas kernels  39.7 us (94%)
  local copies, waits for them, and re-layouts  1.59 us (4%)
  between operations  0.66 us (2%)
    pallas_call x1, Pallas kernels, per_device(): pl.pallas_call(functools.partial(kernel, frames, videos, chunks), out_sha...  39.7 us
    unnamed x1, local copies, waits for them, and re-layouts  1.59 us

profile of v3, /device:TPU:0, one launch (start us, length us, event | category | flops | bytes accessed | tf_op | source)
XLA Modules:
  0.0 41.9 jit_solution(12116231125068691785)
XLA Ops:
  0.7 39.7 %shard_map.109 = bf16[1,1,320,256]{3,2,1,0:T(8,128)(2,1)} custom-call(s32[1]{0:T(128)S(6)} %copy.13.steps_hbm, s32[2,4]{1,0:T(2,128)} %match_hbm.1, s32[2,2,2,4]{3,2,1,0:T(2,128)} %bitcast.5, bf16[1,1,320,256]{3,2,1,0:T(8,128)(2,1)} %bitcast.4, bf16[3,3,320,320]{3,2,1,0:T(8,128)(2,1)} %conv_a_hbm.1, bf16[3,3,320,320]{3,2,1,0:T(8,128)(2,1)} %conv_b_hbm.1, ...), custom_call_target="tpu_custom_call" | custom-call | tf_op jit(solution)/shard_map/pallas_call | solution.py:583
  40.3 1.6 %copy.14 = bf16[1,1,256,320]{2,3,1,0:T(8,128)(2,1)} copy(bf16[1,1,256,320]{2,3,1,0:T(8,128)(2,1)} %bitcast.3) | data formatting | bytes 327680

commit v4 on v3

--- a/solution.py
+++ b/solution.py
@@ -290,6 +290,14 @@
         )
 
 
+    pl.semaphore_wait(barrier, frames + columns - 1)
+    for d in range(1, frames):
+        time_copy(d).start()
+    for i in (1, 2, 4, 5):
+        local[i].wait()
+    chain_step(0, 0)
+    chain_step(1, 0)
+
     group_width = channels // NORM_GROUPS
     row_group = jnp.floor((iota((channels, channels), 0).astype(F32) + 0.5) / group_width)
     col_group = jnp.floor((iota((channels, channels), 1).astype(F32) + 0.5) / group_width)
@@ -320,21 +328,21 @@
     source = jnp.transpose(xt_ref[...].astype(F32))
     x_ref[...] = source.astype(BF16)
     spread_act(gn_silu(source, same_group, count))
-    for i in (1, 2, 4, 5):
-        local[i].wait()
-    pl.semaphore_wait(barrier, frames + columns - 1)
-    for d in range(1, frames):
-        time_copy(d).start()
-    chain_step(0, 0)
-    chain_step(1, 0)
     local[6].wait()
     inner = convolve(conv_a, 0, tokens)
+    channel_mean = jnp.sum(inner, axis=0, keepdims=True) * (1.0 / tokens)
+    inner = inner - channel_mean
+    channel_spread = jnp.sum(inner * inner, axis=0, keepdims=True)
     chain_step(0, 1)
     bias = time_parts[0, 0:1]
     for d in range(1, frames):
         time_copy(d).wait_recv()
         bias = bias + time_parts[d, 0:1]
-    spread_act(gn_silu(inner + bias, same_group, count))
+    offset = channel_mean + bias
+    offset = offset - group_total(offset, same_group) * (1.0 / group_width)
+    spread = group_total(channel_spread + tokens * (offset * offset), same_group) * (1.0 / count)
+    u = (inner + offset) * (1.0 / jnp.sqrt(spread + EPS))
+    spread_act(u * (1.0 / (1.0 + jnp.exp(-u))))
     chain_step(1, 1)
     local[7].wait()
     half = tokens // 2
@@ -432,10 +440,12 @@
             frame=to,
         )
 
-    def attend(i):
+    def attend(i, between=None):
         part = slice(i * half, (i + 1) * half)
         blocks = [jnp.zeros((half, min(128, channels - s)), F32) for s in range(0, channels, 128)]
         for m in range(2):
+            if m == 1 and between is not None:
+                between()
             target = match_ref[m, video]
             keys = keys_ref[target]
             values = values_ref[target]
@@ -475,19 +485,25 @@
             go_copy(c, d).start()
         recv_blocks[c, frame] = send_blocks[c, frame]
 
-    if chunks == 2:
-        send_out(0, attend(0))
+    def late_hop():
         chain_step(2, 2)
         chain_step(3, 2)
+
+    if chunks == 2:
+        send_out(0, attend(0, late_hop))
+        if frames > 3:
+            chain_step(2, 3)
+            chain_step(3, 3)
         send_out(1, attend(1))
     else:
-        first = attend(0)
-        chain_step(2, 2)
-        chain_step(3, 2)
+        first = attend(0, late_hop)
+        if frames > 3:
+            chain_step(2, 3)
+            chain_step(3, 3)
         second_part = attend(1)
         send_out(0, jnp.concatenate([first, second_part], axis=0))
     for s in range(2, 4):
-        for k in range(3, frames):
+        for k in range(4, frames):
             chain_step(s, k)
     chain_finish(2)
     chain_finish(3)

time: 42.1 us -> 44.6 us (1.059)
  Pallas kernels: 39.7 us -> 42.2 us
    pallas_call x1, Pallas kernels: 39.7 us -> 42.2 us  [per_device(): pl.pallas_call(functools.partial(kernel, frames, videos, chunks), out_sha...]
where the time goes in v4:
time: 44.6 us; the launch traced here: 44.4 us
  Pallas kernels  42.2 us (95%)
  local copies, waits for them, and re-layouts  1.59 us (4%)
  between operations  0.66 us (1%)
    pallas_call x1, Pallas kernels, per_device(): pl.pallas_call(functools.partial(kernel, frames, videos, chunks), out_sha...  42.2 us
    unnamed x1, local copies, waits for them, and re-layouts  1.59 us

profile of v4, /device:TPU:0, one launch (start us, length us, event | category | flops | bytes accessed | tf_op | source)
XLA Modules:
  0.0 44.4 jit_solution(6090138047788085891)
XLA Ops:
  0.7 42.2 %shard_map.109 = bf16[1,1,320,256]{3,2,1,0:T(8,128)(2,1)} custom-call(s32[1]{0:T(128)S(6)} %copy.13.steps_hbm, s32[2,4]{1,0:T(2,128)} %match_hbm.1, s32[2,2,2,4]{3,2,1,0:T(2,128)} %bitcast.5, bf16[1,1,320,256]{3,2,1,0:T(8,128)(2,1)} %bitcast.4, bf16[3,3,320,320]{3,2,1,0:T(8,128)(2,1)} %conv_a_hbm.1, bf16[3,3,320,320]{3,2,1,0:T(8,128)(2,1)} %conv_b_hbm.1, ...), custom_call_target="tpu_custom_call" | custom-call | tf_op jit(solution)/shard_map/pallas_call | solution.py:599
  42.8 1.6 %copy.14 = bf16[1,1,256,320]{2,3,1,0:T(8,128)(2,1)} copy(bf16[1,1,256,320]{2,3,1,0:T(8,128)(2,1)} %bitcast.3) | data formatting | bytes 327680

commit v5 on v4

--- a/solution.py
+++ b/solution.py
@@ -290,14 +290,6 @@
         )
 
 
-    pl.semaphore_wait(barrier, frames + columns - 1)
-    for d in range(1, frames):
-        time_copy(d).start()
-    for i in (1, 2, 4, 5):
-        local[i].wait()
-    chain_step(0, 0)
-    chain_step(1, 0)
-
     group_width = channels // NORM_GROUPS
     row_group = jnp.floor((iota((channels, channels), 0).astype(F32) + 0.5) / group_width)
     col_group = jnp.floor((iota((channels, channels), 1).astype(F32) + 0.5) / group_width)
@@ -328,6 +320,13 @@
     source = jnp.transpose(xt_ref[...].astype(F32))
     x_ref[...] = source.astype(BF16)
     spread_act(gn_silu(source, same_group, count))
+    pl.semaphore_wait(barrier, frames + columns - 1)
+    for d in range(1, frames):
+        time_copy(d).start()
+    for i in (1, 2, 4, 5):
+        local[i].wait()
+    chain_step(0, 0)
+    chain_step(1, 0)
     local[6].wait()
     inner = convolve(conv_a, 0, tokens)
     channel_mean = jnp.sum(inner, axis=0, keepdims=True) * (1.0 / tokens)
@@ -371,8 +370,7 @@
         for d in range(1, columns):
             far_copy(d, c).start()
         near_copy(c).start()
-    chain_step(0, 2)
-    chain_step(1, 2)
+        chain_step(c, 2)
     for i in (8, 9, 10, 11, 13, 14):
         local[i].wait()
     for s in range(2):
@@ -490,10 +488,8 @@
         chain_step(3, 2)
 
     if chunks == 2:
-        send_out(0, attend(0, late_hop))
-        if frames > 3:
-            chain_step(2, 3)
-            chain_step(3, 3)
+        send_out(0, attend(0))
+        late_hop()
         send_out(1, attend(1))
     else:
         first = attend(0, late_hop)
@@ -503,7 +499,7 @@
         second_part = attend(1)
         send_out(0, jnp.concatenate([first, second_part], axis=0))
     for s in range(2, 4):
-        for k in range(4, frames):
+        for k in range(3, frames):
             chain_step(s, k)
     chain_finish(2)
     chain_finish(3)

time: 44.6 us -> 42.4 us (0.951)
  Pallas kernels: 42.2 us -> 40 us
    pallas_call x1, Pallas kernels: 42.2 us -> 40 us  [per_device(): pl.pallas_call(functools.partial(kernel, frames, videos, chunks), out_sha...]
where the time goes in v5:
time: 42.4 us; the launch traced here: 42.3 us
  Pallas kernels  40 us (94%)
  local copies, waits for them, and re-layouts  1.59 us (4%)
  between operations  0.66 us (2%)
    pallas_call x1, Pallas kernels, per_device(): pl.pallas_call(functools.partial(kernel, frames, videos, chunks), out_sha...  40 us
    unnamed x1, local copies, waits for them, and re-layouts  1.59 us

profile of v5, /device:TPU:0, one launch (start us, length us, event | category | flops | bytes accessed | tf_op | source)
XLA Modules:
  0.0 42.3 jit_solution(15973958173182092775)
XLA Ops:
  0.7 40.0 %shard_map.109 = bf16[1,1,320,256]{3,2,1,0:T(8,128)(2,1)} custom-call(s32[1]{0:T(128)S(6)} %copy.13.steps_hbm, s32[2,4]{1,0:T(2,128)} %match_hbm.1, s32[2,2,2,4]{3,2,1,0:T(2,128)} %bitcast.5, bf16[1,1,320,256]{3,2,1,0:T(8,128)(2,1)} %bitcast.4, bf16[3,3,320,320]{3,2,1,0:T(8,128)(2,1)} %conv_a_hbm.1, bf16[3,3,320,320]{3,2,1,0:T(8,128)(2,1)} %conv_b_hbm.1, ...), custom_call_target="tpu_custom_call" | custom-call | tf_op jit(solution)/shard_map/pallas_call | solution.py:595
  40.7 1.6 %copy.14 = bf16[1,1,256,320]{2,3,1,0:T(8,128)(2,1)} copy(bf16[1,1,256,320]{2,3,1,0:T(8,128)(2,1)} %bitcast.3) | data formatting | bytes 327680
